TPU v7x, 128 devices: a whole 4x4x4 slice. The times are simulated.
128 devices in a mesh: seq: 8 (over y_lo, x), samp: 16 (over y_hi, z, core).
Axes of the slice: x: 4, y: 4 (y_hi: 2, y_lo: 2; y = y_hi * 2 + y_lo), z: 4, core: 2. Of those that a mesh axis runs over, the one named last changes fastest.
Arguments:
- prompt_ids: int32 [2048], replicated, may hold values from 0 to 64127
- comp_ids: int32 [64, 2], replicated, may hold values from 0 to 64127
- prefix_len: int32 [1], replicated, may hold values from 8192 to 16384
- prompt_offset: int32 [1], replicated, may hold values from 16384 to 32768
- embed_table: bfloat16 [64128, 8192], P('seq', 'samp'), may hold values from -3 to 3
- attn_gain: bfloat16 [8192], P('samp'), may hold values from 0.099609375 to 1.8984375
- query_key_value_weight: bfloat16 [8192, 10240], P('samp', 'seq')
- w_out: bfloat16 [8192, 8192], P('seq', 'samp'), may hold values from -0.29882812 to 0.29882812
- key_value_cache: bfloat16 [2, 8, 16384, 128], P(None, 'seq'), may hold values from -6 to 6
Outputs:
- prompt_out: bfloat16 [2048, 8192], P('seq', 'samp')
- comp_out: bfloat16 [64, 2, 8192], P('seq', None, 'samp')
Inputs may be any that keep to these rules, and one draw needn't show every extreme that they name: The valid cache slots are slots 0 to prefix_len - 1. The valid cache slots hold the positions directly before prompt_offset.
All inputs are finite; a program needn't handle non-finite values.
Results may differ from a plain program's by a relative error of at most 0.03.
Values may be sent and summed in bfloat16 or wider, within the bound.
No kernel may reach another device: no remote copies, remote signals or barrier semaphores. Data moves between devices by JAX's collectives and lax.ppermute only.
A program may use at most 192 MiB of HBM per device.

v0:
```python
import math
import jax
import jax.numpy as jnp
from jax import lax
from jax.sharding import PartitionSpec as P

NORM_EPS = 1e-05
MASK_FILL = -1e30


def from_everyone(shard, axis):
    copies = jnp.broadcast_to(shard, (lax.axis_size(axis), *shard.shape))
    return lax.all_to_all(copies, axis, split_axis=0, concat_axis=0, tiled=True)


def of_everyone(shard, axis):
    return from_everyone(shard, axis).sum(axis=0)


def sent_together(arrays, axis, dim, along):
    both = jnp.concatenate(arrays, axis=along)
    filled, at, outs = (lax.all_gather(both, axis, axis=dim, tiled=True), 0, [])
    for a in arrays:
        outs.append(lax.slice_in_dim(filled, at, at + a.shape[along], axis=along))
        at += a.shape[along]
    return tuple(outs)


def in_blocks(shard, dim, length):
    shape = shard.shape
    parts = shard.reshape(*shape[:dim], length, shape[dim] // length, *shape[dim + 1 :])
    return jnp.moveaxis(parts, dim, 0)


def sent_and_summed(shard, axis, dim):
    length = lax.axis_size(axis)
    parts = lax.all_to_all(in_blocks(shard, dim, length), axis, 0, 0, tiled=True)
    return jnp.sum(parts.astype(jnp.float32), axis=0)


def rope_freqs(head_dim):
    half_dim = head_dim // 2
    dim_index = jnp.arange(half_dim, dtype=jnp.float32)
    base_freq = 1.0 / jnp.power(500000.0, 2.0 * dim_index / head_dim)
    wavelength = 2.0 * math.pi / base_freq
    blend = (8192.0 / wavelength - 1.0) / 3.0
    middle = (1.0 - blend) * base_freq / 8.0 + blend * base_freq
    return jnp.where(
        wavelength > 8192.0, base_freq / 8.0, jnp.where(wavelength < 2048.0, base_freq, middle)
    )


def rotate(vectors, positions):
    angles = positions[:, None] * rope_freqs(vectors.shape[-1])[None, :]
    bcast_shape = (angles.shape[0],) + (1,) * (vectors.ndim - 2) + (angles.shape[1],)
    cosine = jnp.cos(angles).reshape(bcast_shape)
    sine_vals = jnp.sin(angles).reshape(bcast_shape)
    half_dim = vectors.shape[-1] // 2
    first_half = vectors[..., :half_dim]
    second_half = vectors[..., half_dim:]
    return jnp.concatenate(
        [
            first_half * cosine - second_half * sine_vals,
            second_half * cosine + first_half * sine_vals,
        ],
        axis=-1,
    )


def absorb(running, queries, key_block, value_block, live_mask, key_form):
    run_max, run_sum, run_acc = running
    score_scale = 1.0 / math.sqrt(queries.shape[-1])
    scores = (
        jnp.einsum(
            "rgqd," + key_form + "->rgqk", queries, key_block, preferred_element_type=jnp.float32
        )
        * score_scale
    )
    live_wide = live_mask[:, None, None, :]
    scores = jnp.where(live_wide, scores, MASK_FILL)
    new_max = jnp.maximum(run_max, jnp.max(scores, axis=-1))
    weights = jnp.where(live_wide, jnp.exp(scores - new_max[..., None]), 0.0)
    factor = jnp.exp(run_max - new_max)
    run_sum = run_sum * factor + jnp.sum(weights, axis=-1)
    run_acc = run_acc * factor[..., None] + jnp.einsum(
        "rgqk," + key_form + "->rgqd",
        weights.astype(jnp.bfloat16),
        value_block,
        preferred_element_type=jnp.float32,
    )
    return (new_max, run_sum, run_acc)


def seq_order(row_block, samp_count, seq_count, own_prompt, own_comp):
    row_width = row_block.shape[1]
    blocks = row_block.reshape(samp_count, own_prompt + own_comp, row_width)
    prompt_part = blocks[:, :own_prompt].reshape(
        seq_count, samp_count * own_prompt // seq_count, row_width
    )
    comp_part = blocks[:, own_prompt:].reshape(
        seq_count, samp_count * own_comp // seq_count, row_width
    )
    return jnp.concatenate([prompt_part, comp_part], axis=1).reshape(-1, row_width)


def body(
    prompt_ids,
    comp_ids,
    prefix_len,
    prompt_offset,
    embed_table,
    attn_gain,
    query_key_value_weight,
    w_out,
    key_value_cache,
):
    seq_count = lax.axis_size("seq")
    samp_count = lax.axis_size("samp")
    seq_index = lax.axis_index("seq")
    samp_index = lax.axis_index("samp")
    prompt_len = prompt_ids.shape[0]
    comp_count, new_len = comp_ids.shape
    vocab_rows, local_width = embed_table.shape
    group_dev = key_value_cache.shape[1]
    cache_len = key_value_cache.shape[2]
    head_dim = key_value_cache.shape[3]
    columns = query_key_value_weight.shape[1]
    heads_per = columns // (group_dev * head_dim) - 2
    own_prompt = prompt_len // samp_count
    own_comp = comp_count * new_len // samp_count
    own_rows = own_prompt + own_comp
    arranged = jnp.concatenate(
        [prompt_ids.reshape(samp_count, own_prompt), comp_ids.reshape(samp_count, own_comp)], axis=1
    ).reshape(-1)
    local_ids = arranged - seq_index * vocab_rows
    inside = (local_ids >= 0) & (local_ids < vocab_rows)
    picked = jnp.take(embed_table, jnp.clip(local_ids, 0, vocab_rows - 1), axis=0)
    partial_rows = jnp.where(inside[:, None], picked, jnp.zeros((), jnp.bfloat16))
    embedded = lax.psum(partial_rows, "seq").astype(jnp.float32).astype(jnp.bfloat16)
    wide = embedded.astype(jnp.float32)
    square_sums = of_everyone(jnp.sum(wide * wide, axis=1), "samp")
    inv_rms = lax.rsqrt(square_sums / (local_width * samp_count) + NORM_EPS)
    normalized_rows = (wide * inv_rms[:, None] * attn_gain.astype(jnp.float32)[None, :]).astype(
        jnp.bfloat16
    )
    own_features = lax.all_to_all(normalized_rows, "samp", split_axis=0, concat_axis=1, tiled=True)
    projected_rows = jnp.dot(
        own_features,
        lax.all_gather(query_key_value_weight, "samp", axis=0, tiled=True),
        preferred_element_type=jnp.float32,
    )
    start_pos = prompt_offset[0]
    own_prompt_pos = start_pos + samp_index * own_prompt + jnp.arange(own_prompt, dtype=jnp.int32)
    own_comp_pos = start_pos + prompt_len + jnp.arange(own_comp, dtype=jnp.int32) % new_len
    own_pos = jnp.concatenate([own_prompt_pos, own_comp_pos]).astype(jnp.float32)
    shaped = projected_rows.reshape(own_rows, group_dev, heads_per + 2, head_dim)
    queries = rotate(shaped[:, :, :heads_per], own_pos).astype(jnp.bfloat16)
    key_rows = rotate(shaped[:, :, heads_per], own_pos).astype(jnp.bfloat16)
    value_rows = shaped[:, :, heads_per + 1].astype(jnp.bfloat16)
    running = (
        jnp.full((own_rows, group_dev, heads_per), MASK_FILL, jnp.float32),
        jnp.zeros((own_rows, group_dev, heads_per), jnp.float32),
        jnp.zeros((own_rows, group_dev, heads_per, head_dim), jnp.float32),
    )
    prefix_count = prefix_len[0]
    block_len = min(cache_len, 2048)

    def cache_step(block_index, running_in):
        first_slot = block_index * block_len
        cache_block = lax.dynamic_slice(
            key_value_cache, (0, 0, first_slot, 0), (2, group_dev, block_len, head_dim)
        )
        slot_ids = first_slot + jnp.arange(block_len, dtype=jnp.int32)
        live_mask = jnp.broadcast_to((slot_ids < prefix_count)[None, :], (own_rows, block_len))
        return absorb(running_in, queries, cache_block[0], cache_block[1], live_mask, "gkd")

    running = lax.fori_loop(0, cache_len // block_len, cache_step, running)
    row_ids = jnp.arange(own_rows, dtype=jnp.int32)
    comp_key_ids = jnp.arange(own_comp, dtype=jnp.int32)
    row_local = row_ids - own_prompt
    comp_live = (
        (row_ids[:, None] >= own_prompt)
        & (comp_key_ids[None, :] // new_len == row_local[:, None] // new_len)
        & (comp_key_ids[None, :] % new_len <= row_local[:, None] % new_len)
    )
    running = absorb(
        running, queries, key_rows[own_prompt:], value_rows[own_prompt:], comp_live, "kgd"
    )
    row_prompt = jnp.where(row_ids < own_prompt, samp_index * own_prompt + row_ids, prompt_len)
    piece_keys, piece_values = sent_together(
        (key_rows[:own_prompt], value_rows[:own_prompt]), "samp", 0, 1
    )
    key_pos = jnp.arange(piece_keys.shape[0], dtype=jnp.int32)
    live_mask = key_pos[None, :] <= row_prompt[:, None]
    running = absorb(running, queries, piece_keys, piece_values, live_mask, "kgd")
    run_max, run_sum, run_acc = running
    context = (
        (run_acc / run_sum[..., None])
        .astype(jnp.bfloat16)
        .reshape(own_rows, group_dev * heads_per * head_dim)
    )
    out_rows = prompt_len // seq_count + comp_count * new_len // seq_count
    terms = jnp.dot(
        lax.all_gather(context, "samp", axis=0, tiled=True),
        w_out,
        preferred_element_type=jnp.float32,
    )
    summed = sent_and_summed(
        seq_order(terms, samp_count, seq_count, own_prompt, own_comp).astype(jnp.bfloat16), "seq", 0
    )
    residual = lax.dynamic_slice_in_dim(
        seq_order(embedded, samp_count, seq_count, own_prompt, own_comp),
        seq_index * out_rows,
        out_rows,
        0,
    )
    total = summed + residual.astype(jnp.float32)
    prompt_rows = prompt_len // seq_count
    prompt_out = total[:prompt_rows].astype(jnp.bfloat16)
    comp_out = (
        total[prompt_rows:]
        .reshape(comp_count // seq_count, new_len, local_width)
        .astype(jnp.bfloat16)
    )
    return (prompt_out, comp_out)


def solution(mesh):
    placed = (
        P(),
        P(),
        P(),
        P(),
        P("seq", "samp"),
        P("samp"),
        P("samp", "seq"),
        P("seq", "samp"),
        P(None, "seq", None, None),
    )
    return jax.shard_map(
        body,
        mesh=mesh,
        in_specs=placed,
        out_specs=(P("seq", "samp"), P("seq", None, "samp")),
        check_vma=False,
    )
```

profile of v0, /device:TPU:6, one launch (start us, length us, event | category | flops | bytes accessed | tf_op | source)
XLA Modules:
  0.0 450.5 jit_solution(9055723753952659364)
XLA Ops:
  8.1 0.8 copy.26
  10.8 11.6 %gather_fusion = bf16[2176,512]{1,0:T(8,128)(2,1)S(1)} fusion(bf16[8016,512]{1,0:T(8,128)(2,1)} %param.15, s32[3072]{0:T(1024)S(1)} %pad_clamp_fusion), kind=kCustom, calls=%fused_computation | custom fusion | bytes 4465152 | tf_op jit(solution)/shard_map/jit(_take)/gather | solution.py:137
  22.4 2.8 select_select_fusion
  25.9 84.2 %all-reduce.2.cloned.1.call-done = bf16[2176,512]{1,0:T(8,128)(2,1)} async-done(((bf16[2176,512]{1,0:T(8,128)(2,1)}), bf16[2176,512]{1,0:T(8,128)(2,1)}) %all-reduce.2.cloned.1.call-update) | async-done | bytes 2228240 | tf_op jit(solution)/shard_map/psum | solution.py:139
  110.1 2.1 fusion.26
  112.2 0.7 broadcast_in_dim.154
  113.0 6.9 %all-to-all-start = ((f32[16,1,2176]{2,1,0:T(1,128)}), f32[16,1,2176]{2,1,0:T(1,128)S(1)}, u32[]{:S(2)}, u32[]{:S(2)}) async-start(f32[16,1,2176]{2,1,0:T(1,128)} %broadcast_in_dim.154), calls=%async_computation | async-start | bytes 278528 | tf_op jit(solution)/shard_map/all_to_all | solution.py:13
  119.9 10.1 %all-to-all-done = f32[16,1,2176]{2,1,0:T(1,128)S(1)} async-done(((f32[16,1,2176]{2,1,0:T(1,128)}), f32[16,1,2176]{2,1,0:T(1,128)S(1)}, u32[]{:S(2)}, u32[]{:S(2)}) %all-to-all-start) | async-done | bytes 139296 | tf_op jit(solution)/shard_map/all_to_all | solution.py:13
  130.1 3.6 fusion.28
  133.7 3.7 all-to-all-start.1
  138.6 0.9 iota_compare_fusion
  139.6 51.7 %all-to-all-done.1 = bf16[16,136,512]{2,1,0:T(8,128)(2,1)S(1)} async-done(((bf16[16,136,512]{2,1,0:T(8,128)(2,1)}), bf16[16,136,512]{2,1,0:T(8,128)(2,1)S(1)}, u32[]{:S(2)}, u32[]{:S(2)}) %all-to-all-start.1) | async-done | bytes 2228256 | tf_op jit(solution)/shard_map/all_to_all | solution.py:146
  191.3 2.1 copy.28
  193.5 3.6 reshape.686
  197.0 12.0 %all-gather.4.cloned.1.call-done = bf16[8192,1280]{1,0:T(8,128)(2,1)} async-done(((bf16[512,1280]{1,0:T(8,128)(2,1)}), bf16[8192,1280]{1,0:T(8,128)(2,1)}) %all-gather.4.cloned.1.call-update) | async-done | bytes 20971536 | tf_op jit(solution)/shard_map/all_gather | solution.py:149
  209.0 26.8 %copy.29 = bf16[1280,8192]{1,0:T(8,128)(2,1)} copy(bf16[1280,8192]{0,1:T(8,128)(2,1)} %bitcast.260) | data formatting | bytes 41943040 | tf_op jit(solution)/shard_map/dot_general | solution.py:147
  235.8 10.7 %fusion.83 = (bf16[136,1,10,128]{3,0,2,1:T(8,128)(2,1)S(1)}, f32[136,1,10,128]{3,0,2,1:T(8,128)S(1)}) fusion(bf16[136,8192,1]{1,0,2:T(8,128)(2,1)S(1)} %reshape.686, bf16[10,128,8192]{2,1,0:T(8,128)(2,1)} %bitcast.259), kind=kOutput, calls=%fused_computation.144 | convolution fusion | flops 2852300800 | bytes 24244224 | tf_op jit(solution)/shard_map/dot_general | solution.py:147
  247.9 0.7 fusion.58
  248.9 1.5 subtract_convert_fusion
  250.5 80.6 %while.18 = (s32[]{:T(128)}, f32[136,1,8]{0,2,1:T(8,128)S(1)}, f32[136,1,8]{0,2,1:T(8,128)S(1)}, f32[136,1,8,128]{3,0,2,1:T(8,128)}, s32[]{:T(128)}, /*index=5*/...) while((s32[]{:T(128)}, f32[136,1,8]{0,2,1:T(8,128)S(1)}, ...), condition=%wide.region_6.7_spmd.clone, body=%wide.region_3.6_spmd.clone.sunk | while | flops 1170246016 | bytes 33724172 | solution.py:177
  251.2 2.6 bitcast_reduce_fusion.2
  253.9 2.3 fusion.95
  256.3 3.5 fusion.96
  259.9 0.8 copy-done.6
  261.3 2.6 bitcast_reduce_fusion.2
  264.0 2.3 fusion.95
  266.3 3.5 fusion.96
  269.9 0.8 copy-done.6
  271.4 2.6 bitcast_reduce_fusion.2
  274.0 2.3 fusion.95
  276.4 3.5 fusion.96
  280.0 0.8 copy-done.6
  281.4 2.7 bitcast_reduce_fusion.2
  284.1 2.3 fusion.95
  286.5 3.5 fusion.96
  290.1 0.8 copy-done.6
  291.5 2.6 bitcast_reduce_fusion.2
  294.2 2.3 fusion.95
  296.5 3.5 fusion.96
  300.1 0.8 copy-done.6
  301.6 2.6 bitcast_reduce_fusion.2
  304.2 2.3 fusion.95
  306.6 3.5 fusion.96
  310.2 0.8 copy-done.6
  311.6 2.6 bitcast_reduce_fusion.2
  314.3 2.3 fusion.95
  316.7 3.5 fusion.96
  320.2 0.8 copy-done.6
  321.7 2.6 bitcast_reduce_fusion.2
  324.4 2.3 fusion.95
  326.7 3.5 fusion.96
  330.3 0.8 copy-done.6
  331.5 2.9 fusion.23
  334.4 3.1 fusion.24
  337.6 1.1 fusion.40
  338.7 2.4 fusion.46
  341.1 0.8 copy.34
  341.9 53.3 %all-gather.8.cloned.1.call-done = bf16[2176,1024]{1,0:T(8,128)(2,1)} async-done(((bf16[136,1024]{1,0:T(8,128)(2,1)}), bf16[2176,1024]{1,0:T(8,128)(2,1)}) %all-gather.8.cloned.1.call-update) | async-done | bytes 4456464 | tf_op jit(solution)/shard_map/all_gather | solution.py:204
  395.2 4.7 %convolution_convert_fusion = bf16[2176,512]{1,0:T(8,128)(2,1)S(1)} fusion(bf16[2176,1024]{1,0:T(8,128)(2,1)} %all-gather.8.cloned.1.call-done, bf16[1024,512]{1,0:T(8,128)(2,1)S(1)} %copy-done), kind=kOutput, calls=%fused_computation.37 | convolution fusion | flops 2282815488 | bytes 7733248 | tf_op jit(solution)/shard_map/dot_general | solution.py:203
  400.2 1.6 pad_maximum_fusion
  401.8 4.8 %all-to-all-start.2 = ((bf16[8,272,512]{2,1,0:T(8,128)(2,1)}), bf16[8,272,512]{2,1,0:T(8,128)(2,1)}, u32[]{:S(2)}, u32[]{:S(2)}) async-start(bf16[8,272,512]{2,1,0:T(8,128)(2,1)} %pad_maximum_fusion), calls=%async_computation.2 | async-start | bytes 4456448 | tf_op jit(solution)/shard_map/all_to_all | solution.py:37
  407.0 32.4 %all-to-all-done.2 = bf16[8,272,512]{2,1,0:T(8,128)(2,1)} async-done(((bf16[8,272,512]{2,1,0:T(8,128)(2,1)}), bf16[8,272,512]{2,1,0:T(8,128)(2,1)}, u32[]{:S(2)}, u32[]{:S(2)}) %all-to-all-start.2) | async-done | bytes 2228256 | tf_op jit(solution)/shard_map/all_to_all | solution.py:37
  439.5 2.0 convert_reduce_fusion
  441.6 0.7 slice.115
  (123 shorter events, 12.2 us)
Async XLA Ops:
  8.0 387.2 %copy-start = (bf16[1024,512]{1,0:T(8,128)(2,1)S(1)}, bf16[1024,512]{1,0:T(8,128)(2,1)}, u32[]{:S(2)}) copy-start(bf16[1024,512]{1,0:T(8,128)(2,1)} %param.18) | copy-start | bytes 3145732
  8.0 102.1 %all-reduce.2.cloned.1.call-start = ((), (), s32[]{:S(2)}) async-start(), calls=%async_computation.3 | async-start | bytes 4456448 | tf_op jit(solution)/shard_map/psum | solution.py:139
  22.4 97.4 %copy-start.8 = (bf16[512]{0:T(512)(128)(2,1)S(1)}, bf16[512]{0:T(512)(128)(2,1)}, u32[]{:S(2)}) copy-start(bf16[512]{0:T(512)(128)(2,1)} %param.16) | copy-start | bytes 3076
  25.3 183.7 %all-gather.4.cloned.1.call-start = ((), (), s32[]{:S(2)}) async-start(), calls=%async_computation.4 | async-start | bytes 22282240 | tf_op jit(solution)/shard_map/all_gather | solution.py:149
  113.0 17.0 %all-to-all-start = ((f32[16,1,2176]{2,1,0:T(1,128)}), f32[16,1,2176]{2,1,0:T(1,128)S(1)}, u32[]{:S(2)}, u32[]{:S(2)}) async-start(f32[16,1,2176]{2,1,0:T(1,128)} %broadcast_in_dim.154), calls=%async_computation | async-start | bytes 278528 | tf_op jit(solution)/shard_map/all_to_all | solution.py:13
  133.7 57.7 %all-to-all-start.1 = ((bf16[16,136,512]{2,1,0:T(8,128)(2,1)}), bf16[16,136,512]{2,1,0:T(8,128)(2,1)S(1)}, u32[]{:S(2)}, u32[]{:S(2)}) async-start(bf16[16,136,512]{2,1,0:T(8,128)(2,1)} %bitcast.264), calls=%async_computation.1 | async-start | bytes 4456448 | tf_op jit(solution)/shard_map/all_to_all | solution.py:146
  137.4 194.1 %all-gather.6.cloned.1.call-start = ((), (), s32[]{:S(2)}) async-start(), calls=%async_computation.5 | async-start | bytes 1114112 | tf_op jit(solution)/shard_map/all_gather | solution.py:22
  246.6 0.7 copy-start.4
  246.6 1.0 copy-start.2
  248.6 146.6 %all-gather.8.cloned.1.call-start = ((), (), s32[]{:S(2)}) async-start(), calls=%async_computation.6 | async-start | bytes 4734976 | tf_op jit(solution)/shard_map/all_gather | solution.py:204
  250.5 81.0 %copy-start.3 = (pred[136,2048]{1,0:T(8,128)(4,1)S(1)}, pred[136,2048]{1,0:T(8,128)(4,1)}, u32[]{:S(2)}) copy-start(pred[136,2048]{1,0:T(8,128)(4,1)} %iota_compare_fusion) | copy-start | bytes 835588
  253.9 2.4 copy-start.5
  259.8 0.8 copy-start.6
  264.0 2.4 copy-start.5
  269.9 0.8 copy-start.6
  274.0 2.4 copy-start.5
  279.9 0.8 copy-start.6
  284.1 2.4 copy-start.5
  290.0 0.8 copy-start.6
  294.2 2.4 copy-start.5
  300.1 0.8 copy-start.6
  304.2 2.4 copy-start.5
  310.1 0.8 copy-start.6
  314.3 2.4 copy-start.5
  320.2 0.8 copy-start.6
  324.4 2.4 copy-start.5
  330.3 0.8 copy-start.6
  334.4 3.2 copy-start.7
  334.4 4.3 copy-start.9
  400.2 6.4 %copy-start.1 = (bf16[2176,512]{1,0:T(8,128)(2,1)S(1)}, bf16[2176,512]{1,0:T(8,128)(2,1)}, u32[]{:S(2)}) copy-start(bf16[2176,512]{1,0:T(8,128)(2,1)} %all-reduce.2.cloned.1.call-done) | copy-start | bytes 6684676
  401.8 37.7 %all-to-all-start.2 = ((bf16[8,272,512]{2,1,0:T(8,128)(2,1)}), bf16[8,272,512]{2,1,0:T(8,128)(2,1)}, u32[]{:S(2)}, u32[]{:S(2)}) async-start(bf16[8,272,512]{2,1,0:T(8,128)(2,1)} %pad_maximum_fusion), calls=%async_computation.2 | async-start | bytes 4456448 | tf_op jit(solution)/shard_map/all_to_all | solution.py:37
Sparse Core Ops, SparseCore 0:
  25.4 84.6 all-reduce.1
Sparse Core Ops, SparseCore 1:
  28.3 180.7 all-gather.3
  248.7 42.1 all-gather.5
  342.0 53.1 all-gather.7
where the time goes:
time: 453 us; the launch traced here: 451 us
  waiting for transfers between devices  244 us (54%)
  matrix products  71.7 us (16%)
  local copies, waits for them, and re-layouts  56.1 us (12%)
  other arithmetic  45.4 us (10%)
  between operations  16.7 us (4%)
  starting transfers between devices  15.7 us (3%)
    psum x1, waiting for transfers between devices, body(): lax.psum(partial_rows, 'seq').astype(jnp.float32).astype(jnp.bfloat16)  84.2 us
    all_gather x1, waiting for transfers between devices, body(): lax.all_gather(context, 'samp', axis=0, tiled=True)  53.3 us
    all_to_all x1, waiting for transfers between devices, body(): lax.all_to_all(normalized_rows, 'samp', split_axis=0, concat_axis=1, tile...  51.7 us
    all_to_all x1, waiting for transfers between devices, sent_and_summed(): lax.all_to_all(in_blocks(shard, dim, length), axis, 0, 0, tiled=True)  32.4 us
    dot_general x10, matrix products, absorb(): jnp.einsum('rgqk,' + key_form + '->rgqd', weights.astype(jnp.bfloat16), v...  31.8 us
    dot_general x1, local copies, waits for them, and re-layouts, body(): jnp.dot(own_features, lax.all_gather(query_key_value_weight, 'samp', axis...  26.8 us
    dot_general x10, matrix products, absorb(): jnp.einsum('rgqd,' + key_form + '->rgqk', queries, key_block, preferred_e...  24.4 us
    reduce_sum x10, other arithmetic, absorb(): run_sum = run_sum * factor + jnp.sum(weights, axis=-1)  21.9 us
  transfers between devices with their start and end apart: 7, of which 6 were waited for; matrix products, arithmetic and copies ran while one was open for 20% of the time, Pallas kernels for 0%

commit v1 on v0

--- a/solution.py
+++ b/solution.py
@@ -136,7 +136,11 @@
     inside = (local_ids >= 0) & (local_ids < vocab_rows)
     picked = jnp.take(embed_table, jnp.clip(local_ids, 0, vocab_rows - 1), axis=0)
     partial_rows = jnp.where(inside[:, None], picked, jnp.zeros((), jnp.bfloat16))
-    embedded = lax.psum(partial_rows, "seq").astype(jnp.float32).astype(jnp.bfloat16)
+    embedded = (
+        jnp.sum(lax.all_gather(partial_rows, "seq"), axis=0)
+        .astype(jnp.float32)
+        .astype(jnp.bfloat16)
+    )
     wide = embedded.astype(jnp.float32)
     square_sums = of_everyone(jnp.sum(wide * wide, axis=1), "samp")
     inv_rms = lax.rsqrt(square_sums / (local_width * samp_count) + NORM_EPS)

time: 453 us -> 607 us (1.34)
  waiting for transfers between devices: 244 us -> 387 us
  other arithmetic: 45.4 us -> 52.3 us
    all_gather x0 -> x1, waiting for transfers between devices: none -> 180 us  [body(): lax.all_gather(partial_rows, 'seq')]
    psum x1 -> x0, waiting for transfers between devices: 84.2 us -> none  [body(): lax.psum(partial_rows, 'seq').astype(jnp.float32).astype(jnp.bfloat16)]
    all_gather x1, waiting for transfers between devices: 12 us -> 76.8 us  [body(): lax.all_gather(query_key_value_weight, 'samp', axis=0, tiled=True)]
    all_to_all x1, waiting for transfers between devices: 51.7 us -> 33.8 us  [body(): lax.all_to_all(normalized_rows, 'samp', split_axis=0, concat_axis=1, tile...]
    reduce_sum x0 -> x1, other arithmetic: none -> 9.52 us  [body(): jnp.sum(lax.all_gather(partial_rows, 'seq'), axis=0).astype(jnp.float32)]
  transfers between devices with their start and end apart: 7 -> 7, of which waited for: 6 -> 6; matrix products, arithmetic and copies ran while one was open for 20% -> 17% of each run, Pallas kernels for 0% -> 0%
where the time goes in v1:
time: 607 us; the launch traced here: 605 us
  waiting for transfers between devices  387 us (64%)
  matrix products  73.7 us (12%)
  local copies, waits for them, and re-layouts  60.1 us (10%)
  other arithmetic  52.3 us (9%)
  starting transfers between devices  16.3 us (3%)
  between operations  14.9 us (2%)
    all_gather x1, waiting for transfers between devices, body(): lax.all_gather(partial_rows, 'seq')  180 us
    all_gather x1, waiting for transfers between devices, body(): lax.all_gather(query_key_value_weight, 'samp', axis=0, tiled=True)  76.8 us
    all_gather x1, waiting for transfers between devices, body(): lax.all_gather(context, 'samp', axis=0, tiled=True)  53.6 us
    all_to_all x1, waiting for transfers between devices, body(): lax.all_to_all(normalized_rows, 'samp', split_axis=0, concat_axis=1, tile...  33.8 us
    all_to_all x1, waiting for transfers between devices, sent_and_summed(): lax.all_to_all(in_blocks(shard, dim, length), axis, 0, 0, tiled=True)  32.5 us
    dot_general x10, matrix products, absorb(): jnp.einsum('rgqk,' + key_form + '->rgqd', weights.astype(jnp.bfloat16), v...  31.8 us
    dot_general x1, local copies, waits for them, and re-layouts, body(): jnp.dot(own_features, lax.all_gather(query_key_value_weight, 'samp', axis...  26.8 us
    dot_general x10, matrix products, absorb(): jnp.einsum('rgqd,' + key_form + '->rgqk', queries, key_block, preferred_e...  25.7 us
  transfers between devices with their start and end apart: 7, of which 6 were waited for; matrix products, arithmetic and copies ran while one was open for 17% of the time, Pallas kernels for 0%

profile of v1, /device:TPU:6, one launch (start us, length us, event | category | flops | bytes accessed | tf_op | source)
XLA Modules:
  0.0 605.3 jit_solution(16725234878786681303)
XLA Ops:
  7.2 0.8 copy.25
  8.2 0.7 compare_and_fusion
  8.9 0.7 fusion.64
  10.0 11.6 %gather_fusion = bf16[2176,512]{1,0:T(8,128)(2,1)S(1)} fusion(bf16[8016,512]{1,0:T(8,128)(2,1)} %param.15, s32[3072]{0:T(1024)S(1)} %pad_clamp_fusion), kind=kCustom, calls=%fused_computation | custom fusion | bytes 4465152 | tf_op jit(solution)/shard_map/jit(_take)/gather | solution.py:137
  21.6 2.8 fusion.30
  24.5 0.7 all-gather.7.cloned.1.call-update
  25.2 179.8 %all-gather.5.cloned.1.call-done = bf16[8,2176,512]{2,1,0:T(8,128)(2,1)} async-done(((bf16[1,2176,512]{2,1,0:T(8,128)(2,1)}), bf16[8,2176,512]{2,1,0:T(8,128)(2,1)}) %all-gather.5.cloned.1.call-update) | async-done | bytes 17825808 | tf_op jit(solution)/shard_map/all_gather | solution.py:140
  205.0 9.5 %reduce_sum.76 = bf16[2176,512]{1,0:T(8,128)(2,1)S(1)} reduce(bf16[8,2176,512]{2,1,0:T(8,128)(2,1)} %all-gather.5.cloned.1.call-done, bf16[]{:T(256)} %constant.170.clone.1), dimensions={0}, to_apply=%region_0.1 | reduce | flops 7798784 | bytes 20054018 | tf_op jit(solution)/shard_map/reduce_sum | solution.py:140
  215.0 0.7 broadcast_in_dim.154
  215.8 6.7 %all-to-all-start = ((f32[16,1,2176]{2,1,0:T(1,128)}), f32[16,1,2176]{2,1,0:T(1,128)S(1)}, u32[]{:S(2)}, u32[]{:S(2)}) async-start(f32[16,1,2176]{2,1,0:T(1,128)} %broadcast_in_dim.154), calls=%async_computation | async-start | bytes 278528 | tf_op jit(solution)/shard_map/all_to_all | solution.py:13
  222.5 10.1 %all-to-all-done = f32[16,1,2176]{2,1,0:T(1,128)S(1)} async-done(((f32[16,1,2176]{2,1,0:T(1,128)}), f32[16,1,2176]{2,1,0:T(1,128)S(1)}, u32[]{:S(2)}, u32[]{:S(2)}) %all-to-all-start) | async-done | bytes 139296 | tf_op jit(solution)/shard_map/all_to_all | solution.py:13
  232.8 2.0 multiply_convert_fusion
  234.8 4.4 all-to-all-start.1
  241.1 0.9 iota_compare_fusion
  242.0 33.8 %all-to-all-done.1 = bf16[16,136,512]{2,1,0:T(8,128)(2,1)} async-done(((bf16[16,136,512]{2,1,0:T(8,128)(2,1)}), bf16[16,136,512]{2,1,0:T(8,128)(2,1)}, u32[]{:S(2)}, u32[]{:S(2)}) %all-to-all-start.1) | async-done | bytes 2228256 | tf_op jit(solution)/shard_map/all_to_all | solution.py:150
  275.8 3.8 copy.27
  279.6 4.8 reshape.745
  284.4 76.8 %all-gather.7.cloned.1.call-done = bf16[8192,1280]{1,0:T(8,128)(2,1)} async-done(((bf16[512,1280]{1,0:T(8,128)(2,1)}), bf16[8192,1280]{1,0:T(8,128)(2,1)}) %all-gather.7.cloned.1.call-update) | async-done | bytes 20971536 | tf_op jit(solution)/shard_map/all_gather | solution.py:153
  361.1 26.8 %copy.28 = bf16[1280,8192]{1,0:T(8,128)(2,1)} copy(bf16[1280,8192]{0,1:T(8,128)(2,1)} %bitcast.266) | data formatting | bytes 41943040 | tf_op jit(solution)/shard_map/dot_general | solution.py:151
  387.9 11.4 %fusion.81 = (bf16[136,1,10,128]{3,0,2,1:T(8,128)(2,1)S(1)}, f32[136,1,10,128]{3,0,2,1:T(8,128)S(1)}) fusion(bf16[136,8192,1]{1,0,2:T(8,128)(2,1)} %reshape.745, bf16[10,128,8192]{2,1,0:T(8,128)(2,1)} %bitcast.262), kind=kOutput, calls=%fused_computation.142 | convolution fusion | flops 2852300800 | bytes 24244224 | tf_op jit(solution)/shard_map/dot_general | solution.py:151
  399.3 0.9 copy-done.1
  401.2 0.7 fusion.56
  402.1 1.5 subtract_convert_fusion
  403.7 0.7 copy-done.2
  404.5 80.7 %while.18 = (s32[]{:T(128)}, f32[136,1,8]{0,2,1:T(8,128)}, f32[136,1,8]{0,2,1:T(8,128)}, f32[136,1,8,128]{3,0,2,1:T(8,128)}, s32[]{:T(128)}, /*index=5*/bf16[2,1...) while((s32[]{:T(128)}, f32[136,1,8]{0,2,1:T(8,128)}, ...), condition=%wide.region_6.7_spmd.clone, body=%wide.region_3.6_spmd.clone.sunk | while | flops 1170246016 | bytes 33776480 | solution.py:181
  405.2 2.7 bitcast_reduce_fusion.2
  407.9 2.3 fusion.93
  410.3 3.5 fusion.94
  413.9 0.7 copy.43
  415.3 2.6 bitcast_reduce_fusion.2
  418.0 2.3 fusion.93
  420.4 3.5 fusion.94
  423.9 0.7 copy.43
  425.4 2.6 bitcast_reduce_fusion.2
  428.1 2.3 fusion.93
  430.4 3.5 fusion.94
  435.5 2.7 bitcast_reduce_fusion.2
  438.1 2.3 fusion.93
  440.5 3.5 fusion.94
  445.5 2.6 bitcast_reduce_fusion.2
  448.2 2.3 fusion.93
  450.6 3.5 fusion.94
  455.6 2.6 bitcast_reduce_fusion.2
  458.3 2.3 fusion.93
  460.7 3.5 fusion.94
  465.7 2.6 bitcast_reduce_fusion.2
  468.4 2.3 fusion.93
  470.8 3.5 fusion.94
  475.8 2.6 bitcast_reduce_fusion.2
  478.5 2.3 fusion.93
  480.8 3.5 fusion.94
  485.2 1.4 fusion.82
  486.6 3.2 fusion.23
  489.9 3.1 fusion.24
  493.1 1.1 fusion.38
  494.2 2.4 fusion.44
  496.6 0.7 copy.33
  497.4 53.6 %all-gather.11.cloned.1.call-done = bf16[2176,1024]{1,0:T(8,128)(2,1)} async-done(((bf16[136,1024]{1,0:T(8,128)(2,1)}), bf16[2176,1024]{1,0:T(8,128)(2,1)}) %all-gather.11.cloned.1.call-update) | async-done | bytes 4456464 | tf_op jit(solution)/shard_map/all_gather | solution.py:208
  551.1 4.7 convolution_convert_fusion
  556.0 1.6 pad_maximum_fusion
  557.6 4.8 all-to-all-start.2
  562.8 32.5 %all-to-all-done.2 = bf16[8,272,512]{2,1,0:T(8,128)(2,1)} async-done(((bf16[8,272,512]{2,1,0:T(8,128)(2,1)}), bf16[8,272,512]{2,1,0:T(8,128)(2,1)}, u32[]{:S(2)}, u32[]{:S(2)}) %all-to-all-start.2) | async-done | bytes 2228256 | tf_op jit(solution)/shard_map/all_to_all | solution.py:37
  595.3 2.0 convert_reduce_fusion
  597.4 0.7 slice.115
  (185 shorter events, 15.5 us)
Async XLA Ops:
  7.2 543.9 %copy-start = (bf16[1024,512]{1,0:T(8,128)(2,1)S(1)}, bf16[1024,512]{1,0:T(8,128)(2,1)}, u32[]{:S(2)}) copy-start(bf16[1024,512]{1,0:T(8,128)(2,1)} %param.18) | copy-start | bytes 3145732
  7.2 197.8 %all-gather.5.cloned.1.call-start = ((), (), s32[]{:S(2)}) async-start(), calls=%async_computation.3 | async-start | bytes 20054016 | tf_op jit(solution)/shard_map/all_gather | solution.py:140
  24.4 336.7 %all-gather.7.cloned.1.call-start = ((), (), s32[]{:S(2)}) async-start(), calls=%async_computation.4 | async-start | bytes 22282240 | tf_op jit(solution)/shard_map/all_gather | solution.py:153
  25.2 197.3 %copy-start.17 = (bf16[512]{0:T(512)(128)(2,1)S(1)}, bf16[512]{0:T(512)(128)(2,1)}, u32[]{:S(2)}) copy-start(bf16[512]{0:T(512)(128)(2,1)} %param.16) | copy-start | bytes 3076
  215.8 16.8 %all-to-all-start = ((f32[16,1,2176]{2,1,0:T(1,128)}), f32[16,1,2176]{2,1,0:T(1,128)S(1)}, u32[]{:S(2)}, u32[]{:S(2)}) async-start(f32[16,1,2176]{2,1,0:T(1,128)} %broadcast_in_dim.154), calls=%async_computation | async-start | bytes 278528 | tf_op jit(solution)/shard_map/all_to_all | solution.py:13
  234.8 41.0 %all-to-all-start.1 = ((bf16[16,136,512]{2,1,0:T(8,128)(2,1)}), bf16[16,136,512]{2,1,0:T(8,128)(2,1)}, u32[]{:S(2)}, u32[]{:S(2)}) async-start(bf16[16,136,512]{2,1,0:T(8,128)(2,1)} %multiply_convert_fusion), calls=%async_computation.1 | async-start | bytes 4456448 | tf_op jit(solution)/shard_map/all_to_all | solution.py:150
  239.3 247.4 %all-gather.9.cloned.1.call-start = ((), (), s32[]{:S(2)}) async-start(), calls=%async_computation.5 | async-start | bytes 1114112 | tf_op jit(solution)/shard_map/all_gather | solution.py:22
  399.3 0.9 copy-start.1
  399.3 1.2 copy-start.7
  400.6 0.6 copy-start.11
  400.6 0.6 copy-start.12
  401.9 149.1 %all-gather.11.cloned.1.call-start = ((), (), s32[]{:S(2)}) async-start(), calls=%async_computation.6 | async-start | bytes 4734976 | tf_op jit(solution)/shard_map/all_gather | solution.py:208
  403.6 0.7 copy-start.2
  403.7 0.9 copy-start.3
  405.2 2.7 copy-start.4
  407.9 2.4 copy-start.8
  410.3 3.6 copy-start.13
  413.8 0.8 copy-start.9
  413.9 0.8 copy-start.14
  415.3 2.7 copy-start.4
  418.0 2.4 copy-start.8
  420.3 3.6 copy-start.13
  423.9 0.8 copy-start.9
  423.9 0.8 copy-start.14
  425.4 2.7 copy-start.4
  428.1 2.4 copy-start.8
  430.4 3.5 copy-start.13
  434.0 0.8 copy-start.9
  434.0 0.8 copy-start.14
  435.4 2.7 copy-start.4
  438.1 2.4 copy-start.8
  440.5 3.6 copy-start.13
  444.1 0.8 copy-start.9
  444.1 0.8 copy-start.14
  445.5 2.7 copy-start.4
  448.2 2.4 copy-start.8
  450.6 3.6 copy-start.13
  454.2 0.8 copy-start.9
  454.2 0.8 copy-start.14
  455.6 2.7 copy-start.4
  458.3 2.4 copy-start.8
  460.7 3.5 copy-start.13
  464.2 0.8 copy-start.9
  464.3 0.8 copy-start.14
  465.7 2.7 copy-start.4
  468.4 2.4 copy-start.8
  470.8 3.5 copy-start.13
  474.3 0.8 copy-start.9
  474.3 0.8 copy-start.14
  475.8 2.7 copy-start.4
  478.5 2.4 copy-start.8
  480.8 3.5 copy-start.13
  484.4 0.8 copy-start.9
  484.4 0.8 copy-start.14
  486.6 3.2 copy-start.5
  486.6 3.2 copy-start.6
  489.8 3.1 copy-start.16
  489.8 3.2 copy-start.15
  489.9 3.2 copy-start.10
  489.9 4.3 copy-start.18
  557.6 37.7 %all-to-all-start.2 = ((bf16[8,272,512]{2,1,0:T(8,128)(2,1)}), bf16[8,272,512]{2,1,0:T(8,128)(2,1)}, u32[]{:S(2)}, u32[]{:S(2)}) async-start(bf16[8,272,512]{2,1,0:T(8,128)(2,1)} %pad_maximum_fusion), calls=%async_computation.2 | async-start | bytes 4456448 | tf_op jit(solution)/shard_map/all_to_all | solution.py:37
Sparse Core Ops, SparseCore 0:
  24.5 180.4 all-gather.4
  207.5 153.5 all-gather.6
  402.0 42.3 all-gather.8
  497.5 53.4 all-gather.10
